TPU v7x, 512 devices: a whole 4x8x8 slice. The times are simulated.
512 devices in a mesh: dp: 64 (over z_lo, y, x), seq: 8 (over z_hi, core).
Axes of the slice: x: 4, y: 8, z: 8 (z_hi: 4, z_lo: 2; z = z_hi * 2 + z_lo), core: 2. Of those that a mesh axis runs over, the one named last changes fastest.
Arguments:
- queries: bfloat16 [65536, 4096], P(('dp', 'seq')), may hold values from -48 to 48
- keys: bfloat16 [65536, 1024], P(('dp', 'seq')), may hold values from -6 to 6
- values: bfloat16 [65536, 1024], P(('dp', 'seq')), may hold values from -6 to 6
- out_grad: bfloat16 [65536, 4096], P(('dp', 'seq')), may hold values from -6 to 6
- normed: bfloat16 [65536, 4096], P(('dp', 'seq')), may hold values from -24 to 24
Outputs:
- query_grad: bfloat16 [65536, 4096], P(('dp', 'seq'))
- key_weight_grad: float32 [4096, 1024], P('dp', 'seq')
- value_weight_grad: float32 [4096, 1024], P('dp', 'seq')
All inputs are finite; a program needn't handle non-finite values.
Results may differ from a plain program's by a relative error of at most 0.0055.
Values may be sent and summed in bfloat16 or wider, within the bound.
A program may use at most 128 MiB of HBM per device.

v0:
```python
import math

import jax
import jax.numpy as jnp
from jax import lax
from jax.sharding import PartitionSpec as P

HD = 128


def unrotate(grad, position):
    half = HD // 2
    freqs = jnp.exp(-math.log(500000.0) * (2.0 * jnp.arange(half).astype(jnp.float32) / HD))
    angle = position.astype(jnp.float32)[:, None] * freqs[None, :]
    cosine = jnp.cos(angle)[:, None, :]
    sine = jnp.sin(angle)[:, None, :]
    first = grad[..., :half]
    second = grad[..., half:]
    return jnp.concatenate(
        [first * cosine + second * sine, second * cosine - first * sine], axis=-1
    )


def local(queries, keys, values, out_grad, normed):
    head_q, head_k, head_v, head_g = (
        lax.all_to_all(queries, "seq", split_axis=1, concat_axis=0, tiled=True),
        lax.all_to_all(keys, "seq", split_axis=1, concat_axis=0, tiled=True),
        lax.all_to_all(values, "seq", split_axis=1, concat_axis=0, tiled=True),
        lax.all_to_all(out_grad, "seq", split_axis=1, concat_axis=0, tiled=True),
    )
    length = head_q.shape[0]
    heads = head_q.shape[1] // HD
    kv_heads = head_k.shape[1] // HD
    groups = heads // kv_heads
    scale = 1.0 / math.sqrt(HD)
    block = max(512, length // 8)
    starts = list(range(0, length, block))
    query_parts = [[None] * heads for first in starts]
    high = HD
    key_acc = jnp.zeros((length, HD), jnp.float32)
    value_acc = jnp.zeros((length, HD), jnp.float32)
    for number, first in enumerate(starts):
        last = first + block
        query_pos = first + jnp.arange(block)[:, None]
        key_pos = jnp.arange(last)[None, :]
        allowed = key_pos <= query_pos
        key_block = head_k[:last, 0:high]
        value_block = head_v[:last, 0:high]
        for member in range(groups):
            query_block = head_q[first:last, member * HD : (member + 1) * HD]
            grad_block = head_g[first:last, member * HD : (member + 1) * HD]
            scores = (
                lax.dot_general(
                    query_block,
                    key_block,
                    (((1,), (1,)), ((), ())),
                    preferred_element_type=jnp.float32,
                )
                * scale
            )
            scores = jnp.where(allowed, scores, -jnp.inf)
            top = jnp.max(scores, axis=1, keepdims=True)
            expo = jnp.where(allowed, jnp.exp(scores - top), 0.0)
            probs = expo / jnp.sum(expo, axis=1, keepdims=True)
            probs_b = probs.astype(jnp.bfloat16)
            value_acc = value_acc.at[:last].add(
                lax.dot_general(
                    probs_b,
                    grad_block,
                    (((0,), (0,)), ((), ())),
                    preferred_element_type=jnp.float32,
                )
            )
            prob_grad = lax.dot_general(
                grad_block,
                value_block,
                (((1,), (1,)), ((), ())),
                preferred_element_type=jnp.float32,
            )
            delta = jnp.sum(probs * prob_grad, axis=1, keepdims=True)
            score_grad = (probs * (prob_grad - delta) * scale).astype(jnp.bfloat16)
            query_parts[number][member] = jnp.dot(
                score_grad, key_block, preferred_element_type=jnp.float32
            ).astype(jnp.bfloat16)
            key_acc = key_acc.at[:last].add(
                lax.dot_general(
                    score_grad,
                    query_block,
                    (((0,), (0,)), ((), ())),
                    preferred_element_type=jnp.float32,
                )
            )
    key_groups = [key_acc]
    head_query_grad = jnp.concatenate(
        [jnp.concatenate(parts, axis=1) for parts in query_parts], axis=0
    )
    rows_pos = jnp.arange(length)
    key_total = jnp.stack(key_groups, axis=1)
    key_grad = unrotate(key_total, rows_pos).reshape(length, kv_heads * HD).astype(jnp.bfloat16)
    value_grad = value_acc.astype(jnp.bfloat16)
    query_grad = lax.all_to_all(head_query_grad, "seq", split_axis=0, concat_axis=1, tiled=True)
    width = normed.shape[1]
    piece = lax.all_gather(normed, "seq", axis=0, tiled=True)
    key_part = lax.dot_general(
        piece, key_grad, (((0,), (0,)), ((), ())), preferred_element_type=jnp.float32
    )
    value_part = lax.dot_general(
        piece, value_grad, (((0,), (0,)), ((), ())), preferred_element_type=jnp.float32
    )
    key_full, value_full = lax.psum((key_part, value_part), "dp")
    share = width // lax.axis_size("dp")
    offset = lax.axis_index("dp") * share
    key_weight_grad = lax.dynamic_slice_in_dim(key_full, offset, share, 0)
    value_weight_grad = lax.dynamic_slice_in_dim(value_full, offset, share, 0)
    return (query_grad, key_weight_grad, value_weight_grad)


def solution(mesh):
    placed = (
        P(("dp", "seq"), None),
        P(("dp", "seq"), None),
        P(("dp", "seq"), None),
        P(("dp", "seq"), None),
        P(("dp", "seq"), None),
    )
    return jax.shard_map(
        local,
        mesh=mesh,
        in_specs=placed,
        out_specs=(P(("dp", "seq"), None), P("dp", "seq"), P("dp", "seq")),
        check_vma=False,
    )
```

profile of v0, /device:TPU:6, one launch (start us, length us, event | category | flops | bytes accessed | tf_op | source)
XLA Modules:
  0.0 821.1 jit_solution(14754247701670380773)
XLA Ops:
  7.2 1.9 copy.29
  9.1 10.3 %all-to-all-start.1 = ((bf16[128,8,128]{0,2,1:T(8,128)(2,1)}), bf16[128,8,128]{0,2,1:T(8,128)(2,1)S(1)}, u32[]{:S(2)}, u32[]{:S(2)}) async-start(bf16[128,8,128]{0,2,1:T(8,128)(2,1)} %bitcast.3), calls=%async_computation.1 | async-start | bytes 524288 | tf_op jit(solution)/shard_map/all_to_all | solution.py:27
  19.4 1.8 copy.33
  21.1 11.0 %all-to-all-done.1 = bf16[128,8,128]{0,2,1:T(8,128)(2,1)S(1)} async-done(((bf16[128,8,128]{0,2,1:T(8,128)(2,1)}), bf16[128,8,128]{0,2,1:T(8,128)(2,1)S(1)}, u32[]{:S(2)}, u32[]{:S(2)}) %all-to-all-start.1) | async-done | bytes 262176 | tf_op jit(solution)/shard_map/all_to_all | solution.py:27
  32.1 3.4 all-to-all-start.3
  35.6 1.3 copy.27
  36.9 10.7 %all-to-all-done.3 = bf16[128,8,128]{0,2,1:T(8,128)(2,1)S(1)} async-done(((bf16[128,8,128]{0,2,1:T(8,128)(2,1)}), bf16[128,8,128]{0,2,1:T(8,128)(2,1)S(1)}, u32[]{:S(2)}, u32[]{:S(2)}) %all-to-all-start.3) | async-done | bytes 262176 | tf_op jit(solution)/shard_map/all_to_all | solution.py:28
  47.6 3.6 all-to-all-start
  51.1 1.4 copy.31
  52.5 28.0 %all-to-all-done = bf16[128,8,512]{0,2,1:T(8,128)(2,1)S(1)} async-done(((bf16[128,8,512]{0,2,1:T(8,128)(2,1)}), bf16[128,8,512]{0,2,1:T(8,128)(2,1)S(1)}, u32[]{:S(2)}, u32[]{:S(2)}) %all-to-all-start) | async-done | bytes 1048608 | tf_op jit(solution)/shard_map/all_to_all | solution.py:26
  80.5 3.6 all-to-all-start.2
  87.9 23.6 %all-to-all-done.2 = bf16[128,8,512]{0,2,1:T(8,128)(2,1)S(1)} async-done(((bf16[128,8,512]{0,2,1:T(8,128)(2,1)}), bf16[128,8,512]{0,2,1:T(8,128)(2,1)S(1)}, u32[]{:S(2)}, u32[]{:S(2)}) %all-to-all-start.2) | async-done | bytes 1048608 | tf_op jit(solution)/shard_map/all_to_all | solution.py:29
  121.5 1.8 fusion
  123.4 3.0 fusion.10
  126.4 2.2 multiply_reduce_fusion
  128.6 5.4 multiply_reduce_fusion.3
  138.3 1.8 fusion.44
  142.0 1.3 convolution_add_fusion.1
  143.3 17.6 %all-gather.2.cloned.1.call-done = bf16[1024,4096]{1,0:T(8,128)(2,1)} async-done(((bf16[128,4096]{1,0:T(8,128)(2,1)}), bf16[1024,4096]{1,0:T(8,128)(2,1)}) %all-gather.2.cloned.1.call-update) | async-done | bytes 8388624 | tf_op jit(solution)/shard_map/all_gather | solution.py:103
  160.9 7.2 convolution_bitcast_fusion
  168.0 6.1 convolution_bitcast_fusion.1
  179.8 23.8 %all-to-all-start.4 = ((bf16[8,128,512]{1,2,0:T(8,128)(2,1)}), bf16[8,128,512]{1,2,0:T(8,128)(2,1)S(1)}, u32[]{:S(2)}, u32[]{:S(2)}) async-start(bf16[8,128,512]{1,2,0:T(8,128)(2,1)} %copy_bitcast_fusion), calls=%async_computation.4 | async-start | bytes 2097152 | tf_op jit(solution)/shard_map/all_to_all | solution.py:101
  203.5 33.5 %all-to-all-done.4 = bf16[8,128,512]{1,2,0:T(8,128)(2,1)S(1)} async-done(((bf16[8,128,512]{1,2,0:T(8,128)(2,1)}), bf16[8,128,512]{1,2,0:T(8,128)(2,1)S(1)}, u32[]{:S(2)}, u32[]{:S(2)}) %all-to-all-start.4) | async-done | bytes 1048608 | tf_op jit(solution)/shard_map/all_to_all | solution.py:101
  238.3 572.7 %all-reduce.5.cloned.1.call-done = (f32[4096,128]{0,1:T(8,128)}, f32[4096,128]{0,1:T(8,128)}) async-done(((f32[4096,128]{0,1:T(8,128)}, f32[4096,128]{0,1:T(8,128)}), (f32[4096,128]{0,1:T(8,128)}, f32[4096,128]{0,1:T(8,128)})) %all-reduce.5.cloned.1.call-update) | async-done | bytes 4194320 | tf_op jit(solution)/shard_map/psum | solution.py:110
  (114 shorter events, 29.7 us)
Async XLA Ops:
  7.2 28.4 %copy-start.19 = (bf16[128,4096]{1,0:T(8,128)(2,1)S(1)}, bf16[128,4096]{1,0:T(8,128)(2,1)}, u32[]{:S(2)}) copy-start(bf16[128,4096]{1,0:T(8,128)(2,1)} %param.53) | copy-start | bytes 3145732
  9.1 23.1 %all-to-all-start.1 = ((bf16[128,8,128]{0,2,1:T(8,128)(2,1)}), bf16[128,8,128]{0,2,1:T(8,128)(2,1)S(1)}, u32[]{:S(2)}, u32[]{:S(2)}) async-start(bf16[128,8,128]{0,2,1:T(8,128)(2,1)} %bitcast.3), calls=%async_computation.1 | async-start | bytes 524288 | tf_op jit(solution)/shard_map/all_to_all | solution.py:27
  32.1 15.4 %all-to-all-start.3 = ((bf16[128,8,128]{0,2,1:T(8,128)(2,1)}), bf16[128,8,128]{0,2,1:T(8,128)(2,1)S(1)}, u32[]{:S(2)}, u32[]{:S(2)}) async-start(bf16[128,8,128]{0,2,1:T(8,128)(2,1)} %bitcast.9), calls=%async_computation.3 | async-start | bytes 524288 | tf_op jit(solution)/shard_map/all_to_all | solution.py:28
  35.5 15.6 %copy-start.20 = (bf16[128,4096]{1,0:T(8,128)(2,1)S(1)}, bf16[128,4096]{1,0:T(8,128)(2,1)}, u32[]{:S(2)}) copy-start(bf16[128,4096]{1,0:T(8,128)(2,1)} %param.56) | copy-start | bytes 3145732
  47.6 32.9 %all-to-all-start = ((bf16[128,8,512]{0,2,1:T(8,128)(2,1)}), bf16[128,8,512]{0,2,1:T(8,128)(2,1)S(1)}, u32[]{:S(2)}, u32[]{:S(2)}) async-start(bf16[128,8,512]{0,2,1:T(8,128)(2,1)} %bitcast), calls=%async_computation | async-start | bytes 2097152 | tf_op jit(solution)/shard_map/all_to_all | solution.py:26
  80.5 30.9 %all-to-all-start.2 = ((bf16[128,8,512]{0,2,1:T(8,128)(2,1)}), bf16[128,8,512]{0,2,1:T(8,128)(2,1)S(1)}, u32[]{:S(2)}, u32[]{:S(2)}) async-start(bf16[128,8,512]{0,2,1:T(8,128)(2,1)} %bitcast.6), calls=%async_computation.2 | async-start | bytes 2097152 | tf_op jit(solution)/shard_map/all_to_all | solution.py:29
  84.1 76.8 %all-gather.2.cloned.1.call-start = ((), (), s32[]{:S(2)}) async-start(), calls=%async_computation.5 | async-start | bytes 9437184 | tf_op jit(solution)/shard_map/all_gather | solution.py:103
  84.8 726.2 %all-reduce.5.cloned.1.call-start = ((), (), s32[]{:S(2)}) async-start(), calls=%async_computation.6 | async-start | bytes 8388608 | tf_op jit(solution)/shard_map/psum | solution.py:110
  87.9 33.7 %copy-start.4 = (bf16[8,128,512]{2,1,0:T(8,128)(2,1)}, bf16[8,128,512]{2,1,0:T(8,128)(2,1)S(1)}, u32[]{:S(2)}) copy-start(bf16[8,128,512]{2,1,0:T(8,128)(2,1)S(1)} %copy.28) | copy-start | bytes 3145732
  112.0 5.9 copy-start.16
  118.6 1.2 copy-start.8
  119.4 1.2 copy-start.17
  119.4 1.3 copy-start.18
  134.1 3.8 copy-start.14
  134.1 1.6 copy-start.5
  136.6 1.3 copy-start.2
  137.0 1.3 copy-start.22
  174.1 1.3 copy-start.13
  174.1 1.6 copy-start.11
  175.2 1.1 copy-start.7
  175.2 1.5 copy-start.15
  175.2 1.9 copy-start.3
  175.7 1.9 copy-start.1
  179.8 57.3 %all-to-all-start.4 = ((bf16[8,128,512]{1,2,0:T(8,128)(2,1)}), bf16[8,128,512]{1,2,0:T(8,128)(2,1)S(1)}, u32[]{:S(2)}, u32[]{:S(2)}) async-start(bf16[8,128,512]{1,2,0:T(8,128)(2,1)} %copy_bitcast_fusion), calls=%async_computation.4 | async-start | bytes 2097152 | tf_op jit(solution)/shard_map/all_to_all | solution.py:101
  (6 other events, 5.4 us)
Sparse Core Ops, SparseCore 0:
  87.0 73.7 all-gather.1
  174.3 636.6 all-reduce.4
where the time goes:
time: 826 us; the launch traced here: 821 us
  waiting for transfers between devices  698 us (85%)
  starting transfers between devices  44.7 us (5%)
  matrix products  36.6 us (4%)
  local copies, waits for them, and re-layouts  18.5 us (2%)
  between operations  14.6 us (2%)
  other arithmetic  9.06 us (1%)
    psum x1, waiting for transfers between devices, local(): key_full, value_full = lax.psum((key_part, value_part), 'dp')  573 us
    all_to_all x1, waiting for transfers between devices, local(): lax.all_to_all(head_query_grad, 'seq', split_axis=0, concat_axis=1, tiled...  33.5 us
    all_to_all x1, waiting for transfers between devices, local(): lax.all_to_all(queries, 'seq', split_axis=1, concat_axis=0, tiled=True)  28 us
    all_to_all x1, starting transfers between devices, local(): lax.all_to_all(head_query_grad, 'seq', split_axis=0, concat_axis=1, tiled...  23.8 us
    all_to_all x1, waiting for transfers between devices, local(): lax.all_to_all(out_grad, 'seq', split_axis=1, concat_axis=0, tiled=True)  23.6 us
    all_gather x1, waiting for transfers between devices, local(): piece = lax.all_gather(normed, 'seq', axis=0, tiled=True)  17.6 us
  transfers between devices with their start and end apart: 7, of which 7 were waited for; matrix products, arithmetic and copies ran while one was open for 5% of the time, Pallas kernels for 0%

commit v1 on v0

v1 whole, which is shorter than its diff:
```python
import functools
import math

import jax
import jax.numpy as jnp
import numpy as np
from jax import lax
from jax.experimental import pallas as pl
from jax.experimental.pallas import tpu as pltpu
from jax.sharding import PartitionSpec as P

HD = 128
BLOCK = 256


def rotary_tables(length):
    half = HD // 2
    freqs = np.exp(-math.log(500000.0) * (2.0 * np.arange(half, dtype=np.float32) / HD)).astype(np.float32)
    angle = np.arange(length, dtype=np.float32)[:, None] * freqs[None, :]
    cosine, sine = np.cos(angle), np.sin(angle)
    return (
        np.concatenate([cosine, cosine], axis=1).astype(np.float32),
        np.concatenate([sine, -sine], axis=1).astype(np.float32),
    )


def attention_kernel(q_ref, k_ref, v_ref, g_ref, cos_ref, sin_ref, dq_ref, dkv_ref, dk_acc, dv_acc):
    length = q_ref.shape[0]
    heads = q_ref.shape[1] // HD
    scale = 1.0 / math.sqrt(HD)
    rate = scale * math.log2(math.e)
    dk_acc[...] = jnp.zeros_like(dk_acc)
    dv_acc[...] = jnp.zeros_like(dv_acc)
    for first in range(0, length, BLOCK):
        last = first + BLOCK
        rows = pl.ds(first, BLOCK)

        def step(head, carry, first=first, last=last, rows=rows):
            cols = pl.ds(pl.multiple_of(head * HD, HD), HD)
            q = q_ref[rows, cols]
            g = g_ref[rows, cols]
            k = k_ref[:last, :]
            v = v_ref[:last, :]
            contract_last = (((1,), (1,)), ((), ()))
            s = lax.dot_general(k, q, contract_last, preferred_element_type=jnp.float32)
            key_pos = lax.broadcasted_iota(jnp.int32, s.shape, 0)
            query_pos = lax.broadcasted_iota(jnp.int32, s.shape, 1) + first
            s = jnp.where(key_pos <= query_pos, s, -jnp.inf)
            top = jnp.max(s, axis=0, keepdims=True)
            e = jnp.exp2((s - top) * rate)
            p = e * (1.0 / jnp.sum(e, axis=0, keepdims=True))
            dv_acc[:last, :] += jnp.dot(p.astype(jnp.bfloat16), g, preferred_element_type=jnp.float32)
            dp = lax.dot_general(v, g, contract_last, preferred_element_type=jnp.float32)
            delta = jnp.sum(p * dp, axis=0, keepdims=True)
            ds = (p * ((dp - delta) * scale)).astype(jnp.bfloat16)
            dk_acc[:last, :] += jnp.dot(ds, q, preferred_element_type=jnp.float32)
            dq_ref[rows, cols] = lax.dot_general(
                ds, k, (((0,), (0,)), ((), ())), preferred_element_type=jnp.float32
            ).astype(jnp.bfloat16)
            return carry

        lax.fori_loop(0, heads, step, 0)
    dk = dk_acc[...]
    dk = dk * cos_ref[...] + pltpu.roll(dk, HD // 2, 1) * sin_ref[...]
    dkv_ref[:, :HD] = dk.astype(jnp.bfloat16)
    dkv_ref[:, HD:] = dv_acc[...].astype(jnp.bfloat16)


def attention(q, k, v, g):
    length = q.shape[0]
    cosine, sine = rotary_tables(length)
    vmem = pl.BlockSpec(memory_space=pltpu.VMEM)
    return pl.pallas_call(
        attention_kernel,
        out_shape=(
            jax.ShapeDtypeStruct(q.shape, jnp.bfloat16),
            jax.ShapeDtypeStruct((length, 2 * HD), jnp.bfloat16),
        ),
        in_specs=[vmem] * 6,
        out_specs=(vmem, vmem),
        scratch_shapes=[
            pltpu.VMEM((length, HD), jnp.float32),
            pltpu.VMEM((length, HD), jnp.float32),
        ],
        cost_estimate=pl.CostEstimate(flops=4_000_000_000, bytes_accessed=6_000_000, transcendentals=3_000_000),
        name="attention",
    )(q, k, v, g, jnp.asarray(cosine), jnp.asarray(sine))


def local(queries, keys, values, out_grad, normed):
    q, k, v, g = (
        lax.all_to_all(x, "seq", split_axis=1, concat_axis=0, tiled=True)
        for x in (queries, keys, values, out_grad)
    )
    dq, dkv = attention(q, k, v, g)
    query_grad = lax.all_to_all(dq, "seq", split_axis=0, concat_axis=1, tiled=True)
    gathered = lax.all_gather(normed, "seq", axis=0, tiled=True)
    part = lax.dot_general(
        gathered, dkv, (((0,), (0,)), ((), ())), preferred_element_type=jnp.float32
    ).astype(jnp.bfloat16)
    groups = lax.axis_size("dp")
    parts = lax.all_to_all(
        part.reshape(groups, part.shape[0] // groups, 2 * HD), "dp", split_axis=0, concat_axis=0
    )
    total = jnp.sum(parts.astype(jnp.float32), axis=0)
    return (query_grad, total[:, :HD], total[:, HD:])


def solution(mesh):
    rows = P(("dp", "seq"), None)
    return jax.shard_map(
        local,
        mesh=mesh,
        in_specs=(rows,) * 5,
        out_specs=(rows, P("dp", "seq"), P("dp", "seq")),
        check_vma=False,
    )
```

time: 826 us -> 281 us (0.34)
  waiting for transfers between devices: 698 us -> 147 us
  blocking collectives: 0 us -> 48.4 us
  matrix products: 36.6 us -> 5.94 us
  Pallas kernels: 0 us -> 21.4 us
  starting transfers between devices: 44.7 us -> 32.4 us
  other arithmetic: 9.06 us -> 0.31 us
  local copies, waits for them, and re-layouts: 18.5 us -> 9.96 us
    psum x1 -> x0, waiting for transfers between devices: 573 us -> none  [local(): key_full, value_full = lax.psum((key_part, value_part), 'dp')]
    all_to_all x0 -> x1, blocking collectives: none -> 48.4 us  [local(): lax.all_to_all(x, 'seq', split_axis=1, concat_axis=0, tiled=True)]
    all_to_all x5, waiting for transfers between devices: 107 us -> 147 us  [the longest x3 75.5 us: local(): lax.all_to_all(x, 'seq', split_axis=1, concat_axis=0, tiled=True)]
    dot_general x41 -> x1, matrix products: 36.6 us -> 5.94 us  [local(): lax.dot_general(gathered, dkv, (((0,), (0,)), ((), ())), preferred_elemen...]
    pallas_call x0 -> x1, Pallas kernels: none -> 21.4 us  [attention(): pl.pallas_call(attention_kernel, out_shape=(jax.ShapeDtypeStruct(q.shape,...]
    all_gather x1, waiting for transfers between devices: 17.6 us -> 0.02 us  [local(): gathered = lax.all_gather(normed, 'seq', axis=0, tiled=True)]
    unnamed x53 -> x10, local copies, waits for them, and re-layouts: 13.6 us -> 0.91 us
    all_to_all x5, starting transfers between devices: 44.6 us -> 32.4 us  [the longest x3 17.3 us: local(): lax.all_to_all(x, 'seq', split_axis=1, concat_axis=0, tiled=True)]
  transfers between devices with their start and end apart: 7 -> 6, of which waited for: 7 -> 5; matrix products, arithmetic and copies ran while one was open for 5% -> 5% of each run, Pallas kernels for 0% -> 8%
where the time goes in v1:
time: 281 us; the launch traced here: 280 us
  waiting for transfers between devices  147 us (52%)
  blocking collectives  48.4 us (17%)
  starting transfers between devices  32.4 us (12%)
  Pallas kernels  21.4 us (8%)
  between operations  14.1 us (5%)
  local copies, waits for them, and re-layouts  9.96 us (4%)
  matrix products  5.94 us (2%)
    all_to_all x3, waiting for transfers between devices, local(): lax.all_to_all(x, 'seq', split_axis=1, concat_axis=0, tiled=True)  75.5 us
    all_to_all x1, waiting for transfers between devices, local(): lax.all_to_all(part.reshape(groups, part.shape[0] // groups, 2 * HD), 'dp...  50.3 us
    all_to_all x1, blocking collectives, local(): lax.all_to_all(x, 'seq', split_axis=1, concat_axis=0, tiled=True)  48.4 us
    pallas_call x1, Pallas kernels, attention(): pl.pallas_call(attention_kernel, out_shape=(jax.ShapeDtypeStruct(q.shape,...  21.4 us
    all_to_all x1, waiting for transfers between devices, local(): lax.all_to_all(dq, 'seq', split_axis=0, concat_axis=1, tiled=True)  21 us
    all_to_all x3, starting transfers between devices, local(): lax.all_to_all(x, 'seq', split_axis=1, concat_axis=0, tiled=True)  17.3 us
    all_to_all x1, starting transfers between devices, local(): lax.all_to_all(part.reshape(groups, part.shape[0] // groups, 2 * HD), 'dp...  11.5 us
    dot_general x1, matrix products, local(): lax.dot_general(gathered, dkv, (((0,), (0,)), ((), ())), preferred_elemen...  5.94 us
  transfers between devices with their start and end apart: 6, of which 5 were waited for; matrix products, arithmetic and copies ran while one was open for 5% of the time, Pallas kernels for 8%

profile of v1, /device:TPU:6, one launch (start us, length us, event | category | flops | bytes accessed | tf_op | source)
XLA Modules:
  0.0 279.9 jit_solution(15561442479768208033)
XLA Ops:
  7.2 0.7 all-gather.2.cloned.1.call-update
  7.9 0.2 copy-done
  8.1 0.8 copy_bitcast_fusion.3
  8.9 10.3 %all-to-all-start.1 = ((bf16[128,8,128]{2,0,1:T(8,128)(2,1)}), bf16[128,8,128]{2,0,1:T(8,128)(2,1)S(1)}, u32[]{:S(2)}, u32[]{:S(2)}) async-start(bf16[128,8,128]{2,0,1:T(8,128)(2,1)} %copy_bitcast_fusion.3), calls=%async_computation.1 | async-start | bytes 524288 | tf_op jit(solution)/shard_map/all_to_all | solution.py:92
  19.2 1.7 copy_bitcast_fusion.2
  20.9 11.1 %all-to-all-done.1 = bf16[128,8,128]{2,0,1:T(8,128)(2,1)S(1)} async-done(((bf16[128,8,128]{2,0,1:T(8,128)(2,1)}), bf16[128,8,128]{2,0,1:T(8,128)(2,1)S(1)}, u32[]{:S(2)}, u32[]{:S(2)}) %all-to-all-start.1) | async-done | bytes 262176 | tf_op jit(solution)/shard_map/all_to_all | solution.py:92
  31.9 3.4 %all-to-all-start.2 = ((bf16[128,8,128]{2,0,1:T(8,128)(2,1)}), bf16[128,8,128]{2,0,1:T(8,128)(2,1)S(1)}, u32[]{:S(2)}, u32[]{:S(2)}) async-start(bf16[128,8,128]{2,0,1:T(8,128)(2,1)} %copy_bitcast_fusion.2), calls=%async_computation.2 | async-start | bytes 524288 | tf_op jit(solution)/shard_map/all_to_all | solution.py:92
  35.4 2.3 copy.31
  37.6 15.5 %all-to-all-done.2 = bf16[128,8,128]{2,0,1:T(8,128)(2,1)S(1)} async-done(((bf16[128,8,128]{2,0,1:T(8,128)(2,1)}), bf16[128,8,128]{2,0,1:T(8,128)(2,1)S(1)}, u32[]{:S(2)}, u32[]{:S(2)}) %all-to-all-start.2) | async-done | bytes 262176 | tf_op jit(solution)/shard_map/all_to_all | solution.py:92
  53.2 0.7 copy-done.4
  53.8 3.6 %all-to-all-start = ((bf16[128,8,512]{2,0,1:T(8,128)(2,1)}), bf16[128,8,512]{2,0,1:T(8,128)(2,1)S(1)}, u32[]{:S(2)}, u32[]{:S(2)}) async-start(bf16[128,8,512]{2,0,1:T(8,128)(2,1)} %bitcast.38), calls=%async_computation | async-start | bytes 2097152 | tf_op jit(solution)/shard_map/all_to_all | solution.py:92
  57.4 0.1 copy.30
  57.5 48.9 %all-to-all-done = bf16[128,8,512]{2,0,1:T(8,128)(2,1)S(1)} async-done(((bf16[128,8,512]{2,0,1:T(8,128)(2,1)}), bf16[128,8,512]{2,0,1:T(8,128)(2,1)S(1)}, u32[]{:S(2)}, u32[]{:S(2)}) %all-to-all-start) | async-done | bytes 1048608 | tf_op jit(solution)/shard_map/all_to_all | solution.py:92
  106.4 48.4 %all_to_all.100 = bf16[128,8,512]{2,0,1:T(8,128)(2,1)} all-to-all(bf16[128,8,512]{2,0,1:T(8,128)(2,1)S(1)} %bitcast.41), channel_id=1, replica_groups=mesh['dp'=64,'seq'=8] {'seq'}, dimensions={1} | all-to-all | bytes 2097152 | tf_op jit(solution)/shard_map/all_to_all | solution.py:92
  154.8 21.4 %attention.1 = (bf16[1024,512]{1,0:T(8,128)(2,1)}, bf16[1024,256]{1,0:T(8,128)(2,1)}) custom-call(bf16[1024,512]{1,0:T(8,128)(2,1)} %bitcast.45, bf16[1024,128]{1,0:T(8,128)(2,1)} %bitcast.48, bf16[1024,128]{1,0:T(8,128)(2,1)} %bitcast.49, bf16[1024,512]{1,0:T(8,128)(2,1)} %bitcast.47, f32[1024,128]{1,0:T(8,128)} %constant.6.clone.cos_ref, ...), custom_call_target="tpu_custom_call" | custom-call | flops 4000000000 | bytes 6000000 | tf_op jit(solution)/shard_map/attention/pallas_call | solution.py:73
  176.2 3.6 %all-to-all-start.4 = ((bf16[8,128,512]{2,1,0:T(8,128)(2,1)}), bf16[8,128,512]{2,1,0:T(8,128)(2,1)S(1)}, u32[]{:S(2)}, u32[]{:S(2)}) async-start(bf16[8,128,512]{2,1,0:T(8,128)(2,1)} %bitcast.44), calls=%async_computation.4 | async-start | bytes 2097152 | tf_op jit(solution)/shard_map/all_to_all | solution.py:96
  179.8 5.9 %fusion = bf16[4096,256]{0,1:T(8,128)(2,1)S(1)} fusion(bf16[1024,256]{1,0:T(8,128)(2,1)} %get-tuple-element.6, bf16[1024,4096]{1,0:T(8,128)(2,1)} %all-gather.2.cloned.1.call-done), kind=kOutput, calls=%fused_computation.1 | convolution fusion | flops 2148532224 | bytes 11010048 | tf_op jit(solution)/shard_map/dot_general | solution.py:98
  185.7 2.5 copy.20
  188.2 21.0 %all-to-all-done.4 = bf16[8,128,512]{2,1,0:T(8,128)(2,1)S(1)} async-done(((bf16[8,128,512]{2,1,0:T(8,128)(2,1)}), bf16[8,128,512]{2,1,0:T(8,128)(2,1)S(1)}, u32[]{:S(2)}, u32[]{:S(2)}) %all-to-all-start.4) | async-done | bytes 1048608 | tf_op jit(solution)/shard_map/all_to_all | solution.py:96
  209.3 11.5 %all-to-all-start.5 = ((bf16[64,64,256]{2,1,0:T(8,128)(2,1)}), bf16[64,64,256]{2,1,0:T(8,128)(2,1)S(1)}, u32[]{:S(2)}, u32[]{:S(2)}) async-start(bf16[64,64,256]{2,1,0:T(8,128)(2,1)} %bitcast.39), calls=%async_computation.5 | async-start | bytes 4194304 | tf_op jit(solution)/shard_map/all_to_all | solution.py:102
  220.8 1.1 copy.25
  221.9 50.3 %all-to-all-done.5 = bf16[64,64,256]{2,1,0:T(8,128)(2,1)S(1)} async-done(((bf16[64,64,256]{2,1,0:T(8,128)(2,1)}), bf16[64,64,256]{2,1,0:T(8,128)(2,1)S(1)}, u32[]{:S(2)}, u32[]{:S(2)}) %all-to-all-start.5) | async-done | bytes 2097184 | tf_op jit(solution)/shard_map/all_to_all | solution.py:102
  272.2 0.3 convert_reduce_fusion
  272.5 0.6 fusion.1
  (10 shorter events, 0.1 us)
Async XLA Ops:
  7.2 1.0 copy-start
  7.2 50.2 %copy-start.1 = (bf16[128,4096]{1,0:T(8,128)(2,1)S(1)}, bf16[128,4096]{1,0:T(8,128)(2,1)}, u32[]{:S(2)}) copy-start(bf16[128,4096]{1,0:T(8,128)(2,1)} %param.10) | copy-start | bytes 3145732
  7.2 172.6 %all-gather.2.cloned.1.call-start = ((), (), s32[]{:S(2)}) async-start(), calls=%async_computation.6 | async-start | bytes 9437184 | tf_op jit(solution)/shard_map/all_gather | solution.py:97
  8.9 23.1 %all-to-all-start.1 = ((bf16[128,8,128]{2,0,1:T(8,128)(2,1)}), bf16[128,8,128]{2,0,1:T(8,128)(2,1)S(1)}, u32[]{:S(2)}, u32[]{:S(2)}) async-start(bf16[128,8,128]{2,0,1:T(8,128)(2,1)} %copy_bitcast_fusion.3), calls=%async_computation.1 | async-start | bytes 524288 | tf_op jit(solution)/shard_map/all_to_all | solution.py:92
  31.9 21.2 %copy-start.3 = (bf16[128,8,128]{2,0,1:T(8,128)(2,1)}, bf16[128,8,128]{2,0,1:T(8,128)(2,1)S(1)}, u32[]{:S(2)}) copy-start(bf16[128,8,128]{2,0,1:T(8,128)(2,1)S(1)} %all-to-all-done.1) | copy-start | bytes 786436
  31.9 21.2 %all-to-all-start.2 = ((bf16[128,8,128]{2,0,1:T(8,128)(2,1)}), bf16[128,8,128]{2,0,1:T(8,128)(2,1)S(1)}, u32[]{:S(2)}, u32[]{:S(2)}) async-start(bf16[128,8,128]{2,0,1:T(8,128)(2,1)} %copy_bitcast_fusion.2), calls=%async_computation.2 | async-start | bytes 524288 | tf_op jit(solution)/shard_map/all_to_all | solution.py:92
  53.2 0.7 copy-start.4
  53.8 52.6 %all-to-all-start = ((bf16[128,8,512]{2,0,1:T(8,128)(2,1)}), bf16[128,8,512]{2,0,1:T(8,128)(2,1)S(1)}, u32[]{:S(2)}, u32[]{:S(2)}) async-start(bf16[128,8,512]{2,0,1:T(8,128)(2,1)} %bitcast.38), calls=%async_computation | async-start | bytes 2097152 | tf_op jit(solution)/shard_map/all_to_all | solution.py:92
  106.4 48.4 %copy-start.2 = (bf16[128,8,512]{2,0,1:T(8,128)(2,1)}, bf16[128,8,512]{2,0,1:T(8,128)(2,1)S(1)}, u32[]{:S(2)}) copy-start(bf16[128,8,512]{2,0,1:T(8,128)(2,1)S(1)} %all-to-all-done) | copy-start | bytes 3145732
  176.2 33.1 %all-to-all-start.4 = ((bf16[8,128,512]{2,1,0:T(8,128)(2,1)}), bf16[8,128,512]{2,1,0:T(8,128)(2,1)S(1)}, u32[]{:S(2)}, u32[]{:S(2)}) async-start(bf16[8,128,512]{2,1,0:T(8,128)(2,1)} %bitcast.44), calls=%async_computation.4 | async-start | bytes 2097152 | tf_op jit(solution)/shard_map/all_to_all | solution.py:96
  209.3 62.9 %all-to-all-start.5 = ((bf16[64,64,256]{2,1,0:T(8,128)(2,1)}), bf16[64,64,256]{2,1,0:T(8,128)(2,1)S(1)}, u32[]{:S(2)}, u32[]{:S(2)}) async-start(bf16[64,64,256]{2,1,0:T(8,128)(2,1)} %bitcast.39), calls=%async_computation.5 | async-start | bytes 4194304 | tf_op jit(solution)/shard_map/all_to_all | solution.py:102
Sparse Core Ops, SparseCore 0:
  10.2 125.0 all-gather.1

commit v2 on v1

v2 whole, which is shorter than its diff:
```python
import math

import jax
import jax.numpy as jnp
import numpy as np
from jax import lax
from jax.experimental import pallas as pl
from jax.experimental.pallas import tpu as pltpu
from jax.sharding import PartitionSpec as P

HD = 128
BLOCK = 256


def rotary_tables(length):
    half = HD // 2
    freqs = np.exp(-math.log(500000.0) * (2.0 * np.arange(half, dtype=np.float32) / HD)).astype(np.float32)
    angle = np.arange(length, dtype=np.float32)[:, None] * freqs[None, :]
    cosine, sine = np.cos(angle), np.sin(angle)
    return (
        np.concatenate([cosine, cosine], axis=1).astype(np.float32),
        np.concatenate([sine, -sine], axis=1).astype(np.float32),
    )


BF16 = jnp.bfloat16
F32 = jnp.float32
CHUNKS = 4
GROUP = 8
XS, YS, ZS = 4, 8, 2
MESH = pl.DeviceIdType.MESH


def remote(src, dst, send_sem, recv_sem, device):
    return pltpu.make_async_remote_copy(
        src_ref=src, dst_ref=dst, send_sem=send_sem, recv_sem=recv_sem, device_id=device, device_id_type=MESH
    )


def aligned(index, size):
    return pl.ds(pl.multiple_of(index * size, size), size)


def attend(first, hq, hk, hv, hg, dq, dk_acc, dv_acc, heads):
    scale = 1.0 / math.sqrt(HD)
    rate = scale * math.log2(math.e)
    last = first + BLOCK
    rows = pl.ds(first, BLOCK)
    contract_last = (((1,), (1,)), ((), ()))

    def step(head, carry):
        cols = aligned(head, HD)
        q = hq[rows, cols]
        g = hg[rows, cols]
        k = hk[:last, :]
        v = hv[:last, :]
        s = lax.dot_general(k, q, contract_last, preferred_element_type=F32)
        key_pos = lax.broadcasted_iota(jnp.int32, s.shape, 0)
        query_pos = lax.broadcasted_iota(jnp.int32, s.shape, 1) + first
        s = jnp.where(key_pos <= query_pos, s, -jnp.inf)
        top = jnp.max(s, axis=0, keepdims=True)
        e = jnp.exp2((s - top) * rate)
        p = e * (1.0 / jnp.sum(e, axis=0, keepdims=True))
        dv_acc[:last, :] += jnp.dot(p.astype(BF16), g, preferred_element_type=F32)
        dp = lax.dot_general(v, g, contract_last, preferred_element_type=F32)
        delta = jnp.sum(p * dp, axis=0, keepdims=True)
        ds = (p * ((dp - delta) * scale)).astype(BF16)
        dk_acc[:last, :] += jnp.dot(ds, q, preferred_element_type=F32)
        dq[rows, cols] = lax.dot_general(
            ds, k, (((0,), (0,)), ((), ())), preferred_element_type=F32
        ).astype(BF16)
        return carry

    lax.fori_loop(0, heads, step, 0)


def layer_kernel(
    q_ref, k_ref, v_ref, g_ref, n_ref, cos_ref, sin_ref,
    dq_out, kw_out, vw_out,
    hq, hk, hv, hg, gathered, dq, dk_acc, dv_acc, dkv, part, xrecv, ysend, yrecv, ztotal, zrecv,
    in_send, in_recv, ag_send, ag_recv, dq_send, dq_recv, x_send, x_recv, y_send, y_recv, z_send, z_recv,
):
    tokens, width = n_ref.shape
    length = hq.shape[0]
    heads = hq.shape[1] // HD
    cols = width // CHUNKS
    seq = lax.axis_index("seq")
    dp = lax.axis_index("dp")
    chip, core = seq // 2, seq % 2
    sib = chip * 2 + (1 - core)
    up_chip, down_chip, far_chip = (chip + 1) % 4, (chip + 3) % 4, (chip + 2) % 4
    up, down, far = up_chip * 2 + core, down_chip * 2 + core, far_chip * 2 + core
    zi, yi, xi = dp // (XS * YS), (dp // XS) % YS, dp % XS
    x_peer = [zi * (XS * YS) + yi * XS + (xi + r) % XS for r in range(XS)]
    y_peer = [zi * (XS * YS) + ((yi + r) % YS) * XS + xi for r in range(YS)]
    z_peer = (1 - zi) * (XS * YS) + yi * XS + xi
    peers = [{"seq": (seq + r) % GROUP} for r in range(1, GROUP)]
    peers += [{"dp": x_peer[r]} for r in range(1, XS)]
    peers += [{"dp": y_peer[r]} for r in range(1, YS)]
    peers += [{"dp": z_peer}]

    barrier = pltpu.get_barrier_semaphore()
    for peer in peers:
        pl.semaphore_signal(barrier, inc=1, device_id=peer, device_id_type=MESH)
    pl.semaphore_wait(barrier, len(peers))

    mine = aligned(seq, tokens)
    pairs = ((k_ref, hk), (v_ref, hv), (q_ref, hq), (g_ref, hg))
    sends = []
    enter = []
    for a, (src, dst) in enumerate(pairs):
        piece = dst.shape[1]
        for r in range(1, GROUP):
            to = (seq + r) % GROUP
            copy = remote(
                src.at[:, aligned(to, piece)], dst.at[mine, :],
                in_send.at[a, r - 1], in_recv.at[a, r - 1], {"seq": to},
            )
            copy.start()
            sends.append(copy)
            source = (seq + GROUP - r) % GROUP
            block = dst.at[aligned(source, tokens), :]
            enter.append(remote(block, block, in_send.at[a, r - 1], in_recv.at[a, r - 1], {"seq": to}))

    half = tokens // 2

    def window(block, ch, part_rows=None):
        if part_rows is None:
            rows = aligned(block, tokens)
        else:
            rows = pl.ds(pl.multiple_of(block * tokens + part_rows * half, half), half)
        return gathered.at[rows, pl.ds(ch * cols, cols)]

    def ag(src, dst, ch, kind, to):
        return remote(src, dst, ag_send.at[ch, kind], ag_recv.at[ch, kind], {"seq": to})

    def ag_start(src, dst, ch, kind, to):
        copy = ag(src, dst, ch, kind, to)
        copy.start()
        sends.append(copy)

    def ag_wait(ref, ch, kind):
        ag(ref, ref, ch, kind, sib).wait_recv()

    def own(ch):
        src = n_ref.at[:, pl.ds(ch * cols, cols)]
        for kind, to in ((1, up), (2, down), (0, sib)):
            ag_start(src, window(seq, ch), ch, kind, to)

    def relay(ch):
        ag_wait(window(down, ch), ch, 1)
        ag_start(window(down, ch, 0), window(down, ch, 0), ch, 5, up)
        ag_wait(window(up, ch), ch, 2)
        ag_start(window(up, ch, 1), window(up, ch, 1), ch, 6, down)
        ag_start(window(down, ch), window(down, ch), ch, 3, sib)
        ag_start(window(up, ch), window(up, ch), ch, 4, sib)

    def relay_far(ch):
        ag_wait(window(far, ch, 0), ch, 5)
        ag_start(window(far, ch, 0), window(far, ch, 0), ch, 7, sib)
        ag_wait(window(far, ch, 1), ch, 6)
        ag_start(window(far, ch, 1), window(far, ch, 1), ch, 8, sib)

    def arrived(ch):
        other = 1 - core
        ag_wait(window(sib, ch), ch, 0)
        ag_wait(window(down_chip * 2 + other, ch), ch, 3)
        ag_wait(window(up_chip * 2 + other, ch), ch, 4)
        ag_wait(window(far_chip * 2 + other, ch, 0), ch, 7)
        ag_wait(window(far_chip * 2 + other, ch, 1), ch, 8)

    own(0)
    own(1)

    for src, dst in pairs:
        dst[mine, :] = src[:, aligned(seq, dst.shape[1])]
    gathered[mine, :] = n_ref[...]
    dk_acc[...] = jnp.zeros_like(dk_acc)
    dv_acc[...] = jnp.zeros_like(dv_acc)
    for copy in enter:
        copy.wait_recv()

    attend(0, hq, hk, hv, hg, dq, dk_acc, dv_acc, heads)
    relay(0)
    own(2)
    attend(BLOCK, hq, hk, hv, hg, dq, dk_acc, dv_acc, heads)
    relay_far(0)
    relay(1)
    own(3)
    attend(2 * BLOCK, hq, hk, hv, hg, dq, dk_acc, dv_acc, heads)
    relay_far(1)
    relay(2)
    attend(3 * BLOCK, hq, hk, hv, hg, dq, dk_acc, dv_acc, heads)
    dk = dk_acc[...]
    dk = dk * cos_ref[...] + pltpu.roll(dk, HD // 2, 1) * sin_ref[...]
    dkv[:, :HD] = dk.astype(BF16)
    dkv[:, HD:] = dv_acc[...].astype(BF16)

    share = width // (XS * YS * ZS)

    def weights(ch):
        def step(i, carry):
            at = pl.multiple_of(ch * cols + i * (XS * share), XS * share)
            block = lax.dot_general(
                gathered[:, pl.ds(at, XS * share)], dkv[...], (((0,), (0,)), ((), ())), preferred_element_type=F32
            ).astype(BF16)
            for x in range(XS):
                part[ch, x, i] = block[x * share : (x + 1) * share]
            return carry

        lax.fori_loop(0, cols // (XS * share), step, 0)

    def x_copy(ch, r):
        return remote(
            part.at[ch, (xi + r) % XS], xrecv.at[ch, r - 1],
            x_send.at[ch, r - 1], x_recv.at[ch, r - 1], {"dp": x_peer[r]},
        )

    def scatter_x(ch):
        for r in range(1, XS):
            copy = x_copy(ch, r)
            copy.start()
            sends.append(copy)

    def reduce_x(ch):
        for r in range(1, XS):
            x_copy(ch, r).wait_recv()
        count = cols // (XS * share)
        per = YS // count

        def step(i, carry):
            total = part[ch, xi, i].astype(F32)
            for r in range(1, XS):
                total += xrecv[ch, r - 1, i].astype(F32)
            ysend[(ch % per) * count + i, ch // per] = total.astype(BF16)
            return carry

        lax.fori_loop(0, count, step, 0)

    arrived(0)
    weights(0)
    relay_far(2)
    relay(3)
    scatter_x(0)
    leave = []
    for r in range(1, GROUP):
        to = (seq + r) % GROUP
        width_q = heads * HD
        copy = remote(
            dq.at[aligned(to, tokens), :], dq_out.at[:, aligned(seq, width_q)],
            dq_send.at[r - 1], dq_recv.at[r - 1], {"seq": to},
        )
        copy.start()
        sends.append(copy)
        source = (seq + GROUP - r) % GROUP
        block = dq_out.at[:, aligned(source, width_q)]
        leave.append(remote(block, block, dq_send.at[r - 1], dq_recv.at[r - 1], {"seq": to}))
    dq_out[:, aligned(seq, heads * HD)] = dq[mine, :]
    arrived(1)
    weights(1)
    relay_far(3)
    scatter_x(1)
    reduce_x(0)
    arrived(2)
    weights(2)
    scatter_x(2)
    reduce_x(1)
    arrived(3)
    weights(3)
    scatter_x(3)
    reduce_x(2)
    reduce_x(3)

    def y_copy(r):
        return remote(
            ysend.at[(yi + r) % YS], yrecv.at[r - 1], y_send.at[r - 1], y_recv.at[r - 1], {"dp": y_peer[r]}
        )

    for r in range(1, YS):
        copy = y_copy(r)
        copy.start()
        sends.append(copy)
    for r in range(1, YS):
        y_copy(r).wait_recv()
    for z in range(ZS):
        total = ysend[yi, z].astype(F32)
        for r in range(1, YS):
            total += yrecv[r - 1, z].astype(F32)
        ztotal[z] = total
    last = remote(ztotal.at[1 - zi], zrecv, z_send, z_recv, {"dp": z_peer})
    last.start()
    sends.append(last)
    for copy in leave:
        copy.wait_recv()
    last.wait_recv()
    total = ztotal[zi] + zrecv[...]
    kw_out[...] = total[:, :HD]
    vw_out[...] = total[:, HD:]
    for copy in sends:
        copy.wait_send()


def local(queries, keys, values, out_grad, normed):
    tokens, width = normed.shape
    length = tokens * GROUP
    columns = queries.shape[1] // GROUP
    cosine, sine = rotary_tables(length)
    vmem = pl.BlockSpec(memory_space=pltpu.VMEM)
    share = width // (XS * YS * ZS)
    count = width // CHUNKS // (XS * share)
    dma = pltpu.SemaphoreType.DMA
    return pl.pallas_call(
        layer_kernel,
        out_shape=(
            jax.ShapeDtypeStruct(queries.shape, BF16),
            jax.ShapeDtypeStruct((share, HD), F32),
            jax.ShapeDtypeStruct((share, HD), F32),
        ),
        in_specs=[vmem] * 7,
        out_specs=(vmem,) * 3,
        scratch_shapes=[
            pltpu.VMEM((length, columns), BF16),
            pltpu.VMEM((length, HD), BF16),
            pltpu.VMEM((length, HD), BF16),
            pltpu.VMEM((length, columns), BF16),
            pltpu.VMEM((length, width), BF16),
            pltpu.VMEM((length, columns), BF16),
            pltpu.VMEM((length, HD), F32),
            pltpu.VMEM((length, HD), F32),
            pltpu.VMEM((length, 2 * HD), BF16),
            pltpu.VMEM((CHUNKS, XS, count, share, 2 * HD), BF16),
            pltpu.VMEM((CHUNKS, XS - 1, count, share, 2 * HD), BF16),
            pltpu.VMEM((YS, ZS, share, 2 * HD), BF16),
            pltpu.VMEM((YS - 1, ZS, share, 2 * HD), BF16),
            pltpu.VMEM((ZS, share, 2 * HD), F32),
            pltpu.VMEM((share, 2 * HD), F32),
            dma((4, GROUP - 1)),
            dma((4, GROUP - 1)),
            dma((CHUNKS, 9)),
            dma((CHUNKS, 9)),
            dma((GROUP - 1,)),
            dma((GROUP - 1,)),
            dma((CHUNKS, XS - 1)),
            dma((CHUNKS, XS - 1)),
            dma((YS - 1,)),
            dma((YS - 1,)),
            dma,
            dma,
        ],
        compiler_params=pltpu.CompilerParams(
            collective_id=0, has_side_effects=True, vmem_limit_bytes=56 * 1024 * 1024
        ),
        name="layer",
    )(queries, keys, values, out_grad, normed, jnp.asarray(cosine), jnp.asarray(sine))


def solution(mesh):
    rows = P(("dp", "seq"), None)
    return jax.shard_map(
        local,
        mesh=mesh,
        in_specs=(rows,) * 5,
        out_specs=(rows, P("dp", "seq"), P("dp", "seq")),
        check_vma=False,
    )
```

time: 281 us -> 196 us (0.70)
  Pallas kernels: 21.4 us -> 189 us
  waiting for transfers between devices: 147 us -> 0 us
  blocking collectives: 48.4 us -> 0 us
  starting transfers between devices: 32.4 us -> 0 us
  between operations: 14.1 us -> 0.65 us
  local copies, waits for them, and re-layouts: 9.96 us -> 3.68 us
  matrix products: 5.94 us -> 0 us
    pallas_call x1, Pallas kernels: 21.4 us -> 189 us  [local(): pl.pallas_call(layer_kernel, out_shape=(jax.ShapeDtypeStruct(queries.shap...]
    all_to_all x5 -> x0, waiting for transfers between devices: 147 us -> none  [the longest x3 75.5 us: local(): lax.all_to_all(x, 'seq', split_axis=1, concat_axis=0, tiled=True)]
    all_to_all x1 -> x0, blocking collectives: 48.4 us -> none  [local(): lax.all_to_all(x, 'seq', split_axis=1, concat_axis=0, tiled=True)]
    all_to_all x5 -> x0, starting transfers between devices: 32.4 us -> none  [the longest x3 17.3 us: local(): lax.all_to_all(x, 'seq', split_axis=1, concat_axis=0, tiled=True)]
    dot_general x1 -> x0, matrix products: 5.94 us -> none  [local(): lax.dot_general(gathered, dkv, (((0,), (0,)), ((), ())), preferred_elemen...]
    all_to_all x5 -> x0, local copies, waits for them, and re-layouts: 5.92 us -> none  [the longest x4 4.83 us: local(): lax.all_to_all(x, 'seq', split_axis=1, concat_axis=0, tiled=True)]
  transfers between devices with their start and end apart: 6 -> 0, of which waited for: 5 -> 0; matrix products, arithmetic and copies ran while one was open for 5% -> 0% of each run, Pallas kernels for 8% -> 0%
where the time goes in v2:
time: 196 us; the launch traced here: 193 us
  Pallas kernels  189 us (96%)
  local copies, waits for them, and re-layouts  3.68 us (2%)
    pallas_call x1, Pallas kernels, local(): pl.pallas_call(layer_kernel, out_shape=(jax.ShapeDtypeStruct(queries.shap...  189 us

profile of v2, /device:TPU:6, one launch (start us, length us, event | category | flops | bytes accessed | tf_op | source)
XLA Modules:
  0.0 193.4 jit_solution(1015970750537986004)
XLA Ops:
  0.6 189.0 %layer.1 = (bf16[128,4096]{1,0:T(8,128)(2,1)}, f32[64,128]{1,0:T(8,128)}, f32[64,128]{1,0:T(8,128)}) custom-call(bf16[128,4096]{1,0:T(8,128)(2,1)} %q_ref.1, bf16[128,1024]{1,0:T(8,128)(2,1)} %k_ref.1, bf16[128,1024]{1,0:T(8,128)(2,1)} %v_ref.1, bf16[128,4096]{1,0:T(8,128)(2,1)} %g_ref.1, bf16[128,4096]{1,0:T(8,128)(2,1)} %n_ref.1, ...), custom_call_target="tpu_custom_call" | custom-call | tf_op jit(solution)/shard_map/layer/pallas_call | solution.py:312
  189.7 0.0 copy-start.1
  189.7 2.3 %copy.13 = bf16[128,4096]{1,0:T(8,128)(2,1)} copy(bf16[128,4096]{1,0:T(8,128)(2,1)} %get-tuple-element.6) | data formatting | bytes 2097152
  192.0 0.0 copy-done.1
  192.0 0.0 copy-start
  192.0 0.6 copy.14
  192.6 0.2 copy-done
  192.7 0.6 copy.15
Async XLA Ops:
  189.7 2.3 %copy-start.1 = (f32[64,128]{1,0:T(8,128)S(1)}, f32[64,128]{1,0:T(8,128)}, u32[]{:S(2)}) copy-start(f32[64,128]{1,0:T(8,128)} %get-tuple-element.7) | copy-start | bytes 98308
  192.0 0.8 copy-start

commit v3 on v2

--- a/solution.py
+++ b/solution.py
@@ -25,8 +25,9 @@
 
 BF16 = jnp.bfloat16
 F32 = jnp.float32
-CHUNKS = 4
+CHUNKS = 8
 GROUP = 8
+EARLY = 3
 XS, YS, ZS = 4, 8, 2
 MESH = pl.DeviceIdType.MESH
 
@@ -169,6 +170,14 @@
         ag_wait(window(far_chip * 2 + other, ch, 0), ch, 7)
         ag_wait(window(far_chip * 2 + other, ch, 1), ch, 8)
 
+    def advance(ch):
+        if ch < CHUNKS:
+            relay(ch)
+        if ch + 2 < CHUNKS:
+            own(ch + 2)
+        if ch > 0:
+            relay_far(ch - 1)
+
     own(0)
     own(1)
 
@@ -180,17 +189,10 @@
     for copy in enter:
         copy.wait_recv()
 
-    attend(0, hq, hk, hv, hg, dq, dk_acc, dv_acc, heads)
-    relay(0)
-    own(2)
-    attend(BLOCK, hq, hk, hv, hg, dq, dk_acc, dv_acc, heads)
-    relay_far(0)
-    relay(1)
-    own(3)
-    attend(2 * BLOCK, hq, hk, hv, hg, dq, dk_acc, dv_acc, heads)
-    relay_far(1)
-    relay(2)
-    attend(3 * BLOCK, hq, hk, hv, hg, dq, dk_acc, dv_acc, heads)
+    for number, first in enumerate(range(0, length, BLOCK)):
+        attend(first, hq, hk, hv, hg, dq, dk_acc, dv_acc, heads)
+        if number < EARLY:
+            advance(number)
     dk = dk_acc[...]
     dk = dk * cos_ref[...] + pltpu.roll(dk, HD // 2, 1) * sin_ref[...]
     dkv[:, :HD] = dk.astype(BF16)
@@ -236,57 +238,54 @@
             return carry
 
         lax.fori_loop(0, count, step, 0)
-
-    arrived(0)
-    weights(0)
-    relay_far(2)
-    relay(3)
-    scatter_x(0)
-    leave = []
-    for r in range(1, GROUP):
-        to = (seq + r) % GROUP
-        width_q = heads * HD
-        copy = remote(
-            dq.at[aligned(to, tokens), :], dq_out.at[:, aligned(seq, width_q)],
-            dq_send.at[r - 1], dq_recv.at[r - 1], {"seq": to},
+        for i in range(count):
+            target = (ch % per) * count + i
+
+            @pl.when(target != yi)
+            def _(target=target):
+                y_copy((target + YS - yi) % YS, ch // per, target).start()
+
+    def y_copy(r, z, target):
+        return remote(
+            ysend.at[target, z], yrecv.at[r - 1, z], y_send.at[r - 1, z], y_recv.at[r - 1, z],
+            {"dp": zi * (XS * YS) + target * XS + xi},
         )
-        copy.start()
-        sends.append(copy)
-        source = (seq + GROUP - r) % GROUP
-        block = dq_out.at[:, aligned(source, width_q)]
-        leave.append(remote(block, block, dq_send.at[r - 1], dq_recv.at[r - 1], {"seq": to}))
-    dq_out[:, aligned(seq, heads * HD)] = dq[mine, :]
-    arrived(1)
-    weights(1)
-    relay_far(3)
-    scatter_x(1)
-    reduce_x(0)
-    arrived(2)
-    weights(2)
-    scatter_x(2)
-    reduce_x(1)
-    arrived(3)
-    weights(3)
-    scatter_x(3)
-    reduce_x(2)
-    reduce_x(3)
-
-    def y_copy(r):
-        return remote(
-            ysend.at[(yi + r) % YS], yrecv.at[r - 1], y_send.at[r - 1], y_recv.at[r - 1], {"dp": y_peer[r]}
-        )
-
-    for r in range(1, YS):
-        copy = y_copy(r)
-        copy.start()
-        sends.append(copy)
-    for r in range(1, YS):
-        y_copy(r).wait_recv()
-    for z in range(ZS):
+
+    def reduce_y(z):
+        for r in range(1, YS):
+            y_copy(r, z, (yi + r) % YS).wait_recv()
         total = ysend[yi, z].astype(F32)
         for r in range(1, YS):
             total += yrecv[r - 1, z].astype(F32)
         ztotal[z] = total
+
+    leave = []
+    for ch in range(CHUNKS):
+        if ch + 1 >= EARLY:
+            advance(ch + 1)
+        if ch == CHUNKS - 2:
+            for r in range(1, GROUP):
+                to = (seq + r) % GROUP
+                width_q = heads * HD
+                copy = remote(
+                    dq.at[aligned(to, tokens), :], dq_out.at[:, aligned(seq, width_q)],
+                    dq_send.at[r - 1], dq_recv.at[r - 1], {"seq": to},
+                )
+                copy.start()
+                sends.append(copy)
+                source = (seq + GROUP - r) % GROUP
+                block = dq_out.at[:, aligned(source, width_q)]
+                leave.append(remote(block, block, dq_send.at[r - 1], dq_recv.at[r - 1], {"seq": to}))
+            dq_out[:, aligned(seq, heads * HD)] = dq[mine, :]
+        arrived(ch)
+        weights(ch)
+        scatter_x(ch)
+        if ch > 0:
+            reduce_x(ch - 1)
+        if ch == CHUNKS - 2:
+            reduce_y(0)
+    reduce_x(CHUNKS - 1)
+    reduce_y(1)
     last = remote(ztotal.at[1 - zi], zrecv, z_send, z_recv, {"dp": z_peer})
     last.start()
     sends.append(last)
@@ -296,6 +295,9 @@
     total = ztotal[zi] + zrecv[...]
     kw_out[...] = total[:, :HD]
     vw_out[...] = total[:, HD:]
+    for z in range(ZS):
+        for r in range(1, YS):
+            y_copy(r, z, (yi + r) % YS).wait_send()
     for copy in sends:
         copy.wait_send()
 
@@ -342,8 +344,8 @@
             dma((GROUP - 1,)),
             dma((CHUNKS, XS - 1)),
             dma((CHUNKS, XS - 1)),
-            dma((YS - 1,)),
-            dma((YS - 1,)),
+            dma((YS - 1, ZS)),
+            dma((YS - 1, ZS)),
             dma,
             dma,
         ],

time: 196 us -> 184 us (0.939)
  the two profiles are of different devices: /device:TPU:6 before, /device:TPU:56 now
where the time goes in v3:
time: 184 us
  Pallas kernels  180 us (98%)
  local copies, waits for them, and re-layouts  3.68 us (2%)
    pallas_call x1, Pallas kernels, local(): pl.pallas_call(layer_kernel, out_shape=(jax.ShapeDtypeStruct(queries.shap...  180 us
    unnamed x7, local copies, waits for them, and re-layouts  3.68 us

profile of v3, /device:TPU:56, one launch (start us, length us, event | category | flops | bytes accessed | tf_op | source)
XLA Modules:
  0.0 183.9 jit_solution(9324142704922467080)
XLA Ops:
  0.6 179.5 %layer.1 = (bf16[128,4096]{1,0:T(8,128)(2,1)}, f32[64,128]{1,0:T(8,128)}, f32[64,128]{1,0:T(8,128)}) custom-call(bf16[128,4096]{1,0:T(8,128)(2,1)} %q_ref.1, bf16[128,1024]{1,0:T(8,128)(2,1)} %k_ref.1, bf16[128,1024]{1,0:T(8,128)(2,1)} %v_ref.1, bf16[128,4096]{1,0:T(8,128)(2,1)} %g_ref.1, bf16[128,4096]{1,0:T(8,128)(2,1)} %n_ref.1, ...), custom_call_target="tpu_custom_call" | custom-call | tf_op jit(solution)/shard_map/layer/pallas_call | solution.py:314
  180.2 0.0 copy-start.1
  180.2 2.3 %copy.13 = bf16[128,4096]{1,0:T(8,128)(2,1)} copy(bf16[128,4096]{1,0:T(8,128)(2,1)} %get-tuple-element.6) | data formatting | bytes 2097152
  182.5 0.0 copy-done.1
  182.5 0.0 copy-start
  182.5 0.6 copy.14
  183.1 0.2 copy-done
  183.2 0.6 copy.15
Async XLA Ops:
  180.2 2.3 %copy-start.1 = (f32[64,128]{1,0:T(8,128)S(1)}, f32[64,128]{1,0:T(8,128)}, u32[]{:S(2)}) copy-start(f32[64,128]{1,0:T(8,128)} %get-tuple-element.7) | copy-start | bytes 98308
  182.5 0.8 copy-start
